TPU v7x, 32 devices: a whole 2x2x4 slice. The times are simulated.
32 devices in a mesh: tok: 8 (over z, x), head: 4 (over y, core).
Axes of the slice: x: 2, y: 2, z: 4, core: 2. Of those that a mesh axis runs over, the one named last changes fastest.
Arguments:
- tri_tokens: bfloat16 [4096, 1024], P(('tok', 'head')), may hold values from -6 to 6
- image_tokens: bfloat16 [32768, 1024], P('tok'), may hold values from -6 to 6
- cross_q: bfloat16 [1024, 1024], P(None, 'head'), may hold values from -0.1875 to 0.1875
- cross_kv: bfloat16 [2, 1024, 1024], P(None, None, 'head'), may hold values from -0.1875 to 0.1875
- cross_out: bfloat16 [1024, 1024], P('head'), may hold values from -0.1875 to 0.1875
- self_qkv: bfloat16 [3, 1024, 1024], P(None, None, 'head'), may hold values from -0.1875 to 0.1875
- self_out: bfloat16 [1024, 1024], P('head'), may hold values from -0.1875 to 0.1875
- mlp_in: bfloat16 [1024, 4096], P(None, 'head'), may hold values from -0.1875 to 0.1875
- mlp_out: bfloat16 [4096, 1024], P('head'), may hold values from -0.09375 to 0.09375
Outputs:
- tri_out: bfloat16 [4096, 1024], P(('tok', 'head'))
All inputs are finite; a program needn't handle non-finite values.
Results may differ from a plain program's by a relative error of at most 0.013.
Values may be sent and summed in bfloat16 or wider, within the bound.
A program may use at most 128 MiB of HBM per device.

v0:
```python
import math

import jax
import jax.numpy as jnp
from jax import lax
from jax.sharding import PartitionSpec as P

HEADS = 16


score_gain = 2.5


def layer_norm(values):
    centered = values - jnp.mean(values, axis=-1, keepdims=True)
    return centered * lax.rsqrt(jnp.mean(centered * centered, axis=-1, keepdims=True) + 1e-05)


def head_norm(values, head_count):
    shaped = values.reshape(values.shape[0], head_count, -1)
    normed = shaped * lax.rsqrt(jnp.mean(shaped * shaped, axis=-1, keepdims=True) + 1e-06)
    return normed.reshape(values.shape[0], -1).astype(jnp.bfloat16)


def partial_attention(queries, kv_rows, head_count):
    query_count = queries.shape[0]
    head_size = queries.shape[1] // head_count
    score_scale = score_gain / math.sqrt(head_size)
    query_block = math.gcd(query_count, 512)
    key_block = math.gcd(kv_rows.shape[0], 2048)
    query_blocks = queries.reshape(query_count // query_block, query_block, head_count, head_size)
    key_blocks = kv_rows.reshape(kv_rows.shape[0] // key_block, key_block, 2, head_count, head_size)

    def one_block(query_tile):

        def key_step(running, key_tile):
            weighted, totals = running
            scores = (
                jnp.einsum(
                    "qhd,khd->qhk", query_tile, key_tile[:, 0], preferred_element_type=jnp.float32
                )
                * score_scale
            )
            exp_scores = jnp.exp(scores)
            totals = totals + jnp.sum(exp_scores, axis=-1)
            weighted = weighted + jnp.einsum(
                "qhk,khd->qhd",
                exp_scores.astype(jnp.bfloat16),
                key_tile[:, 1],
                preferred_element_type=jnp.float32,
            )
            return ((weighted, totals), None)

        starting = (
            jnp.zeros((query_block, head_count, head_size), jnp.float32),
            jnp.zeros((query_block, head_count), jnp.float32),
        )
        result, _ = lax.scan(key_step, starting, key_blocks)
        return result

    weighted, totals = lax.map(one_block, query_blocks)
    return (
        weighted.reshape(query_count, head_count, head_size),
        totals.reshape(query_count, head_count),
    )


def finish(weighted, totals):
    return (weighted / totals[:, :, None]).reshape(weighted.shape[0], -1).astype(jnp.bfloat16)


def make_fold(queries, head_count, kv_piece):
    weighted, totals = partial_attention(queries, kv_piece, head_count)
    return (weighted, totals)


def per_device(
    tri_tokens, image_tokens, cross_q, cross_kv, cross_out, self_qkv, self_out, mlp_in, mlp_out
):
    head_width = cross_q.shape[1]
    head_size = tri_tokens.shape[1] // HEADS
    head_count = head_width // head_size

    def spread(normed, project):
        return project(lax.all_gather(normed, "head", axis=0, tiled=True), jnp.int32(0))

    def collect(operand, weight):
        return lax.psum_scatter(
            jnp.dot(operand, weight, preferred_element_type=jnp.float32).astype(jnp.bfloat16),
            "head",
            scatter_dimension=0,
            tiled=True,
        ).astype(jnp.float32)

    def project_cross(shard_rows, first_row):
        return head_norm(
            jnp.dot(shard_rows, cross_q, preferred_element_type=jnp.float32), head_count
        )

    stream_zero = tri_tokens.astype(jnp.float32)
    queries = spread(layer_norm(stream_zero).astype(jnp.bfloat16), project_cross)
    kv_weight = jnp.concatenate([cross_kv[0], cross_kv[1]], axis=1)
    image_kv = jnp.dot(image_tokens, kv_weight, preferred_element_type=jnp.float32)
    view_kv = jnp.concatenate(
        [
            head_norm(image_kv[:, :head_width], head_count),
            image_kv[:, head_width:].astype(jnp.bfloat16),
        ],
        axis=1,
    )
    all_queries = lax.all_gather(queries, "tok", axis=0, tiled=True)
    local_weighted, local_totals = partial_attention(all_queries, view_kv, head_count)
    weighted, totals = (
        lax.psum_scatter(
            local_weighted.astype(jnp.bfloat16), "tok", scatter_dimension=0, tiled=True
        ).astype(jnp.float32),
        lax.psum_scatter(
            local_totals.astype(jnp.bfloat16), "tok", scatter_dimension=0, tiled=True
        ).astype(jnp.float32),
    )
    stream_one = stream_zero + collect(finish(weighted, totals), cross_out)
    self_weight = jnp.concatenate([self_qkv[0], self_qkv[1], self_qkv[2]], axis=1)

    def project_self(shard_rows, first_row):
        mixed = jnp.dot(shard_rows, self_weight, preferred_element_type=jnp.float32)
        return jnp.concatenate(
            [
                head_norm(mixed[:, :head_width], head_count),
                head_norm(mixed[:, head_width : 2 * head_width], head_count),
                mixed[:, 2 * head_width :].astype(jnp.bfloat16),
            ],
            axis=1,
        )

    projected = spread(layer_norm(stream_one).astype(jnp.bfloat16), project_self)
    self_queries = projected[:, :head_width]
    self_kv = projected[:, head_width:]
    weighted, totals = make_fold(
        self_queries, head_count, lax.all_gather(self_kv, "tok", axis=0, tiled=True)
    )
    stream_two = stream_one + collect(finish(weighted, totals), self_out)

    def project_mlp(shard_rows, first_row):
        return jax.nn.gelu(
            jnp.dot(shard_rows, mlp_in, preferred_element_type=jnp.float32), approximate=True
        ).astype(jnp.bfloat16)

    hidden = spread(layer_norm(stream_two).astype(jnp.bfloat16), project_mlp)
    return (stream_two + collect(hidden, mlp_out)).astype(jnp.bfloat16)


def solution(mesh):
    return jax.shard_map(
        per_device,
        mesh=mesh,
        in_specs=(
            P(("tok", "head"), None),
            P("tok", None),
            P(None, "head"),
            P(None, None, "head"),
            P("head", None),
            P(None, None, "head"),
            P("head", None),
            P(None, "head"),
            P("head", None),
        ),
        out_specs=P(("tok", "head"), None),
        check_vma=False,
    )
```

profile of v0, /device:TPU:0, one launch (start us, length us, event | category | flops | bytes accessed | tf_op | source)
XLA Modules:
  0.0 780.1 jit_solution(13781970240689262863)
XLA Ops:
  11.0 19.5 %all-gather.6.cloned.1.call-done = bf16[512,1024]{1,0:T(8,128)(2,1)} async-done(((bf16[128,1024]{1,0:T(8,128)(2,1)}), bf16[512,1024]{1,0:T(8,128)(2,1)}) %all-gather.6.cloned.1.call-update) | async-done | bytes 1048592 | tf_op jit(solution)/shard_map/all_gather | solution.py:85
  33.3 7.1 convolution_bitcast_fusion
  44.0 7.8 %reshape.112 = bf16[2,2048,2,4,64]{1,0,4,3,2:T(2,128)(2,1)} reshape(bf16[4096,512]{0,1:T(8,128)(2,1)} %pad_maximum_fusion) | data formatting | bytes 8388608 | tf_op jit(solution)/shard_map/reshape | solution.py:32
  51.9 6.0 copy.33
  57.9 25.8 %all-gather.8.cloned.1.call-done = bf16[4096,256]{0,1:T(8,128)(2,1)} async-done(((bf16[512,256]{0,1:T(8,128)(2,1)}), bf16[4096,256]{0,1:T(8,128)(2,1)}) %all-gather.8.cloned.1.call-update) | async-done | bytes 2097168 | tf_op jit(solution)/shard_map/all_gather | solution.py:111
  88.2 279.4 %while.48 = (s32[]{:T(128)}, bf16[8,512,4,64]{1,3,2,0:T(8,128)(2,1)}, bf16[8,512,4]{1,2,0:T(4,128)(2,1)S(1)}, bf16[8,512,4,64]{1,3,2,0:T(8,128)(2,1)}, bf16[2,20...) while((s32[]{:T(128)}, bf16[8,512,4,64]{1,3,2,0:T(8,128)(2,1)}, ...), condition=%wide.region_8.9_spmd, body=%wide.region_4.8_spmd.sunk | while | flops 1090783232 | bytes 51168024 | solution.py:61
  89.2 33.2 %while.50 = (s32[]{:T(128)}, f32[512,4,64]{0,2,1:T(8,128)S(1)}, f32[512,4]{0,1:T(4,128)S(1)}, bf16[2,2048,2,4,64]{1,4,3,2,0:T(8,128)(2,1)}, bf16[512,4,64]{0,2,1:T(8,128)(2,1)S(1)}, /*index=5*/s32[]{:T(128)}, s32[]{:T(128)}) while((s32[]{:T(128)}, f32[512,4,64]{0,2,1:T(8,128)S(1)}, f32[512,4]{0,1:T(4,128)S(1)}, ...), condition=%wide.region_7.7_spmd.clone, body=%wide.region_5.6_spmd.clone.sunk | while | flops 1090783232 | bytes 49578100 | solution.py:58
  91.0 7.2 bitcast_reduce_fusion.9
  98.2 7.5 fusion.70
  107.6 7.2 bitcast_reduce_fusion.9
  114.8 7.5 fusion.70
  124.1 33.2 %while.50 = (s32[]{:T(128)}, f32[512,4,64]{0,2,1:T(8,128)S(1)}, f32[512,4]{0,1:T(4,128)S(1)}, bf16[2,2048,2,4,64]{1,4,3,2,0:T(8,128)(2,1)}, bf16[512,4,64]{0,2,1:T(8,128)(2,1)S(1)}, /*index=5*/s32[]{:T(128)}, s32[]{:T(128)}) while((s32[]{:T(128)}, f32[512,4,64]{0,2,1:T(8,128)S(1)}, f32[512,4]{0,1:T(4,128)S(1)}, ...), condition=%wide.region_7.7_spmd.clone, body=%wide.region_5.6_spmd.clone.sunk | while | flops 1090783232 | bytes 49578100 | solution.py:58
  125.9 7.2 bitcast_reduce_fusion.9
  133.1 7.5 fusion.70
  142.5 7.2 bitcast_reduce_fusion.9
  149.7 7.5 fusion.70
  159.0 33.2 %while.50 = (s32[]{:T(128)}, f32[512,4,64]{0,2,1:T(8,128)S(1)}, f32[512,4]{0,1:T(4,128)S(1)}, bf16[2,2048,2,4,64]{1,4,3,2,0:T(8,128)(2,1)}, bf16[512,4,64]{0,2,1:T(8,128)(2,1)S(1)}, /*index=5*/s32[]{:T(128)}, s32[]{:T(128)}) while((s32[]{:T(128)}, f32[512,4,64]{0,2,1:T(8,128)S(1)}, f32[512,4]{0,1:T(4,128)S(1)}, ...), condition=%wide.region_7.7_spmd.clone, body=%wide.region_5.6_spmd.clone.sunk | while | flops 1090783232 | bytes 49578100 | solution.py:58
  160.9 7.2 bitcast_reduce_fusion.9
  168.0 7.5 fusion.70
  177.4 7.2 bitcast_reduce_fusion.9
  184.6 7.5 fusion.70
  193.9 33.2 %while.50 = (s32[]{:T(128)}, f32[512,4,64]{0,2,1:T(8,128)S(1)}, f32[512,4]{0,1:T(4,128)S(1)}, bf16[2,2048,2,4,64]{1,4,3,2,0:T(8,128)(2,1)}, bf16[512,4,64]{0,2,1:T(8,128)(2,1)S(1)}, /*index=5*/s32[]{:T(128)}, s32[]{:T(128)}) while((s32[]{:T(128)}, f32[512,4,64]{0,2,1:T(8,128)S(1)}, f32[512,4]{0,1:T(4,128)S(1)}, ...), condition=%wide.region_7.7_spmd.clone, body=%wide.region_5.6_spmd.clone.sunk | while | flops 1090783232 | bytes 49578100 | solution.py:58
  195.8 7.2 bitcast_reduce_fusion.9
  203.0 7.5 fusion.70
  212.4 7.2 bitcast_reduce_fusion.9
  219.5 7.5 fusion.70
  228.9 33.2 %while.50 = (s32[]{:T(128)}, f32[512,4,64]{0,2,1:T(8,128)S(1)}, f32[512,4]{0,1:T(4,128)S(1)}, bf16[2,2048,2,4,64]{1,4,3,2,0:T(8,128)(2,1)}, bf16[512,4,64]{0,2,1:T(8,128)(2,1)S(1)}, /*index=5*/s32[]{:T(128)}, s32[]{:T(128)}) while((s32[]{:T(128)}, f32[512,4,64]{0,2,1:T(8,128)S(1)}, f32[512,4]{0,1:T(4,128)S(1)}, ...), condition=%wide.region_7.7_spmd.clone, body=%wide.region_5.6_spmd.clone.sunk | while | flops 1090783232 | bytes 49578100 | solution.py:58
  230.7 7.2 bitcast_reduce_fusion.9
  237.9 7.5 fusion.70
  247.3 7.2 bitcast_reduce_fusion.9
  254.5 7.5 fusion.70
  263.8 33.2 %while.50 = (s32[]{:T(128)}, f32[512,4,64]{0,2,1:T(8,128)S(1)}, f32[512,4]{0,1:T(4,128)S(1)}, bf16[2,2048,2,4,64]{1,4,3,2,0:T(8,128)(2,1)}, bf16[512,4,64]{0,2,1:T(8,128)(2,1)S(1)}, /*index=5*/s32[]{:T(128)}, s32[]{:T(128)}) while((s32[]{:T(128)}, f32[512,4,64]{0,2,1:T(8,128)S(1)}, f32[512,4]{0,1:T(4,128)S(1)}, ...), condition=%wide.region_7.7_spmd.clone, body=%wide.region_5.6_spmd.clone.sunk | while | flops 1090783232 | bytes 49578100 | solution.py:58
  265.7 7.2 bitcast_reduce_fusion.9
  272.8 7.5 fusion.70
  282.2 7.2 bitcast_reduce_fusion.9
  289.4 7.5 fusion.70
  298.7 33.2 %while.50 = (s32[]{:T(128)}, f32[512,4,64]{0,2,1:T(8,128)S(1)}, f32[512,4]{0,1:T(4,128)S(1)}, bf16[2,2048,2,4,64]{1,4,3,2,0:T(8,128)(2,1)}, bf16[512,4,64]{0,2,1:T(8,128)(2,1)S(1)}, /*index=5*/s32[]{:T(128)}, s32[]{:T(128)}) while((s32[]{:T(128)}, f32[512,4,64]{0,2,1:T(8,128)S(1)}, f32[512,4]{0,1:T(4,128)S(1)}, ...), condition=%wide.region_7.7_spmd.clone, body=%wide.region_5.6_spmd.clone.sunk | while | flops 1090783232 | bytes 49578100 | solution.py:58
  300.6 7.2 bitcast_reduce_fusion.9
  307.7 7.5 fusion.70
  317.1 7.2 bitcast_reduce_fusion.9
  324.3 7.5 fusion.70
  333.6 33.2 %while.50 = (s32[]{:T(128)}, f32[512,4,64]{0,2,1:T(8,128)S(1)}, f32[512,4]{0,1:T(4,128)S(1)}, bf16[2,2048,2,4,64]{1,4,3,2,0:T(8,128)(2,1)}, bf16[512,4,64]{0,2,1:T(8,128)(2,1)S(1)}, /*index=5*/s32[]{:T(128)}, s32[]{:T(128)}) while((s32[]{:T(128)}, f32[512,4,64]{0,2,1:T(8,128)S(1)}, f32[512,4]{0,1:T(4,128)S(1)}, ...), condition=%wide.region_7.7_spmd.clone, body=%wide.region_5.6_spmd.clone.sunk | while | flops 1090783232 | bytes 49578100 | solution.py:58
  335.5 7.2 bitcast_reduce_fusion.9
  342.6 7.5 fusion.70
  352.1 7.2 bitcast_reduce_fusion.9
  359.2 7.5 fusion.70
  369.0 3.2 copy.48
  372.4 59.1 %reduce-scatter.16.cloned.1.call-done = bf16[512,4]{1,0:T(8,128)(2,1)} async-done(((bf16[4096,4]{1,0:T(8,128)(2,1)}), bf16[512,4]{1,0:T(8,128)(2,1)}) %reduce-scatter.16.cloned.1.call-update) | async-done | bytes 4112
  432.5 70.3 %reduce-scatter.8.cloned.1.call-done = bf16[512,4,64]{0,2,1:T(8,128)(2,1)} async-done(((bf16[4096,4,64]{0,2,1:T(8,128)(2,1)}), bf16[512,4,64]{0,2,1:T(8,128)(2,1)}) %reduce-scatter.8.cloned.1.call-update) | async-done | bytes 262160 | tf_op jit(solution)/shard_map/reduce_scatter | solution.py:114
  505.5 23.7 %reduce-scatter.10.cloned.1.call-done = bf16[128,1024]{1,0:T(8,128)(2,1)} async-done(((bf16[512,1024]{1,0:T(8,128)(2,1)}), bf16[128,1024]{1,0:T(8,128)(2,1)}) %reduce-scatter.10.cloned.1.call-update) | async-done | bytes 262160 | tf_op jit(solution)/shard_map/reduce_scatter | solution.py:88
  535.7 14.5 %all-gather.10.cloned.1.call-done = bf16[512,1024]{1,0:T(8,128)(2,1)} async-done(((bf16[128,1024]{1,0:T(8,128)(2,1)}), bf16[512,1024]{1,0:T(8,128)(2,1)}) %all-gather.10.cloned.1.call-update) | async-done | bytes 1048592 | tf_op jit(solution)/shard_map/all_gather | solution.py:85
  562.7 71.8 %all-gather.12.cloned.1.call-done = bf16[4096,512]{1,0:T(8,128)(2,1)} async-done(((bf16[512,512]{1,0:T(8,128)(2,1)}), bf16[4096,512]{1,0:T(8,128)(2,1)}) %all-gather.12.cloned.1.call-update) | async-done | bytes 4194320 | tf_op jit(solution)/shard_map/all_gather | solution.py:139
  634.4 13.7 %reshape.114 = bf16[2,2048,2,4,64]{4,3,2,1,0:T(4,128)(2,1)} reshape(bf16[4096,512]{1,0:T(8,128)(2,1)} %all-gather.12.cloned.1.call-done) | data formatting | bytes 8388608 | tf_op jit(solution)/shard_map/reshape | solution.py:32
  648.1 12.8 %copy.41 = bf16[2,2048,2,4,64]{1,4,3,2,0:T(8,128)(2,1)} copy(bf16[2,2048,2,4,64]{4,3,2,1,0:T(4,128)(2,1)} %reshape.114) | data formatting | bytes 8388608
  660.9 33.2 %while.49 = (s32[]{:T(128)}, f32[512,4,64]{0,2,1:T(8,128)S(1)}, f32[512,4]{0,1:T(4,128)S(1)}, bf16[2,2048,2,4,64]{1,4,3,2,0:T(8,128)(2,1)}, bf16[512,4,64]{0,2,1:T(8,128)(2,1)S(1)}, /*index=5*/s32[]{:T(128)}, s32[]{:T(128)}) while((s32[]{:T(128)}, f32[512,4,64]{0,2,1:T(8,128)S(1)}, f32[512,4]{0,1:T(4,128)S(1)}, ...), condition=%wide.region_18.19_spmd.clone, body=%wide.region_16.18_spmd.clone.sunk | while | flops 1090783232 | bytes 49578100 | solution.py:58
  662.7 7.2 bitcast_reduce_fusion.8
  669.9 7.5 fusion.68
  679.3 7.2 bitcast_reduce_fusion.8
  686.5 7.5 fusion.68
  694.1 2.5 convolution_convert_fusion.1
  696.7 23.4 %reduce-scatter.12.cloned.1.call-done = bf16[128,1024]{1,0:T(8,128)(2,1)} async-done(((bf16[512,1024]{1,0:T(8,128)(2,1)}), bf16[128,1024]{1,0:T(8,128)(2,1)}) %reduce-scatter.12.cloned.1.call-update) | async-done | bytes 262160 | tf_op jit(solution)/shard_map/reduce_scatter | solution.py:88
  724.3 16.8 %all-gather.14.cloned.1.call-done = bf16[512,1024]{1,0:T(8,128)(2,1)} async-done(((bf16[128,1024]{1,0:T(8,128)(2,1)}), bf16[512,1024]{1,0:T(8,128)(2,1)}) %all-gather.14.cloned.1.call-update) | async-done | bytes 1048592 | tf_op jit(solution)/shard_map/all_gather | solution.py:85
  741.1 5.3 convolution_convert_fusion
  746.5 25.0 %reduce-scatter.14.cloned.1.call-done = bf16[128,1024]{1,0:T(8,128)(2,1)} async-done(((bf16[512,1024]{1,0:T(8,128)(2,1)}), bf16[128,1024]{1,0:T(8,128)(2,1)}) %reduce-scatter.14.cloned.1.call-update) | async-done | bytes 262160 | tf_op jit(solution)/shard_map/reduce_scatter | solution.py:88
  (202 shorter events, 92.4 us)
Async XLA Ops:
  6.5 734.6 %copy-start = (bf16[1024,1024]{1,0:T(8,128)(2,1)S(1)}, bf16[1024,1024]{1,0:T(8,128)(2,1)}, u32[]{:S(2)}) copy-start(bf16[1024,1024]{1,0:T(8,128)(2,1)} %param.23) | copy-start | bytes 6291460
  6.5 24.0 %all-gather.6.cloned.1.call-start = ((), (), s32[]{:S(2)}) async-start(), calls=%async_computation.5 | async-start | bytes 1310720 | tf_op jit(solution)/shard_map/all_gather | solution.py:85
  7.8 25.5 %copy-start.7 = (bf16[2,1024,256]{2,1,0:T(8,128)(2,1)S(1)}, bf16[2,1024,256]{2,1,0:T(8,128)(2,1)}, u32[]{:S(2)}) copy-start(bf16[2,1024,256]{2,1,0:T(8,128)(2,1)} %param.18) | copy-start | bytes 3145732
  10.9 72.7 %all-gather.8.cloned.1.call-start = ((), (), s32[]{:S(2)}) async-start(), calls=%async_computation.6 | async-start | bytes 2359296 | tf_op jit(solution)/shard_map/all_gather | solution.py:111
  33.2 398.3 %reduce-scatter.16.cloned.1.call-start = ((), (), s32[]{:S(2)}) async-start(), calls=%async_computation.14 | async-start | bytes 1179648
  91.0 7.2 copy-start.1
  107.6 7.2 copy-start.1
  125.9 7.2 copy-start.1
  142.5 7.2 copy-start.1
  160.8 7.2 copy-start.1
  177.4 7.2 copy-start.1
  195.8 7.2 copy-start.1
  212.4 7.2 copy-start.1
  230.7 7.2 copy-start.1
  247.3 7.2 copy-start.1
  265.6 7.2 copy-start.1
  282.2 7.2 copy-start.1
  300.5 7.2 copy-start.1
  317.1 7.2 copy-start.1
  335.5 7.2 copy-start.1
  352.1 7.2 copy-start.1
  369.0 133.8 %reduce-scatter.8.cloned.1.call-start = ((), (), s32[]{:S(2)}) async-start(), calls=%async_computation.7 | async-start | bytes 2359296 | tf_op jit(solution)/shard_map/reduce_scatter | solution.py:114
  372.3 131.5 %copy-start.9 = (bf16[256,1024]{1,0:T(8,128)(2,1)S(1)}, bf16[256,1024]{1,0:T(8,128)(2,1)}, u32[]{:S(2)}) copy-start(bf16[256,1024]{1,0:T(8,128)(2,1)} %param.19) | copy-start | bytes 1572868
  372.3 156.9 %copy-start.3 = (bf16[128,1024]{1,0:T(8,128)(2,1)S(1)}, bf16[128,1024]{1,0:T(8,128)(2,1)}, u32[]{:S(2)}) copy-start(bf16[128,1024]{1,0:T(8,128)(2,1)} %param.15) | copy-start | bytes 786436
  372.3 156.9 %reduce-scatter.10.cloned.1.call-start = ((), (), s32[]{:S(2)}) async-start(), calls=%async_computation.8 | async-start | bytes 1310720 | tf_op jit(solution)/shard_map/reduce_scatter | solution.py:88
  505.3 44.9 %all-gather.10.cloned.1.call-start = ((), (), s32[]{:S(2)}) async-start(), calls=%async_computation.9 | async-start | bytes 1310720 | tf_op jit(solution)/shard_map/all_gather | solution.py:85
  533.3 101.1 %all-gather.12.cloned.1.call-start = ((), (), s32[]{:S(2)}) async-start(), calls=%async_computation.10 | async-start | bytes 4718592 | tf_op jit(solution)/shard_map/all_gather | solution.py:139
  552.5 1.3 copy-start.6
  558.6 2.1 copy-start.8
  561.5 158.7 %reduce-scatter.12.cloned.1.call-start = ((), (), s32[]{:S(2)}) async-start(), calls=%async_computation.11 | async-start | bytes 1310720 | tf_op jit(solution)/shard_map/reduce_scatter | solution.py:88
  662.7 7.2 copy-start.2
  679.3 7.2 copy-start.2
  694.0 26.1 %copy-start.4 = (bf16[128,1024]{1,0:T(8,128)(2,1)S(1)}, bf16[128,1024]{1,0:T(8,128)(2,1)}, u32[]{:S(2)}) copy-start(bf16[128,1024]{1,0:T(8,128)(2,1)} %reduce-scatter.10.cloned.1.call-done) | copy-start | bytes 786436
  696.6 44.5 %all-gather.14.cloned.1.call-start = ((), (), s32[]{:S(2)}) async-start(), calls=%async_computation.12 | async-start | bytes 1310720 | tf_op jit(solution)/shard_map/all_gather | solution.py:85
  724.3 47.2 %copy-start.5 = (bf16[128,1024]{1,0:T(8,128)(2,1)S(1)}, bf16[128,1024]{1,0:T(8,128)(2,1)}, u32[]{:S(2)}) copy-start(bf16[128,1024]{1,0:T(8,128)(2,1)} %reduce-scatter.12.cloned.1.call-done) | copy-start | bytes 786436
  724.3 47.1 %reduce-scatter.14.cloned.1.call-start = ((), (), s32[]{:S(2)}) async-start(), calls=%async_computation.13 | async-start | bytes 1310720 | tf_op jit(solution)/shard_map/reduce_scatter | solution.py:88
Sparse Core Ops, SparseCore 0:
  11.1 19.4 all-gather.5
  33.3 50.3 all-gather.7
  369.1 62.3 reduce-scatter.15
  434.9 67.8 reduce-scatter.7
  505.4 23.7 reduce-scatter.9
  533.4 16.6 all-gather.9
  561.6 72.7 all-gather.11
  696.8 23.3 reduce-scatter.11
  724.4 16.6 all-gather.13
  746.6 24.8 reduce-scatter.13
where the time goes:
time: 782 us; the launch traced here: 780 us
  waiting for transfers between devices  350 us (45%)
  matrix products  285 us (36%)
  local copies, waits for them, and re-layouts  106 us (14%)
  other arithmetic  23.7 us (3%)
  between operations  13.8 us (2%)
    dot_general x18, matrix products, key_step(): jnp.einsum('qhk,khd->qhd', exp_scores.astype(jnp.bfloat16), key_tile[:, 1...  136 us
    dot_general x18, matrix products, key_step(): jnp.einsum('qhd,khd->qhk', query_tile, key_tile[:, 0], preferred_element_...  129 us
    reduce_scatter x3, waiting for transfers between devices, collect(): lax.psum_scatter(jnp.dot(operand, weight, preferred_element_type=jnp.floa...  72.1 us
    all_gather x1, waiting for transfers between devices, per_device(): lax.all_gather(self_kv, 'tok', axis=0, tiled=True)  71.8 us
    reduce_scatter x1, waiting for transfers between devices, per_device(): lax.psum_scatter(local_weighted.astype(jnp.bfloat16), 'tok', scatter_dime...  70.3 us
    unnamed x11, waiting for transfers between devices  59.3 us
    all_gather x3, waiting for transfers between devices, spread(): lax.all_gather(normed, 'head', axis=0, tiled=True)  50.9 us
    squeeze x18, local copies, waits for them, and re-layouts, one_block(): result, _ = lax.scan(key_step, starting, key_blocks)  32.9 us
  transfers between devices with their start and end apart: 10, of which 10 were waited for; matrix products, arithmetic and copies ran while one was open for 4% of the time, Pallas kernels for 0%

commit v1 on v0

v1 whole, which is shorter than its diff:
```python
import functools
import math

import jax
import jax.numpy as jnp
from jax import lax
from jax.experimental import pallas as pl
from jax.experimental.pallas import tpu as pltpu
from jax.sharding import PartitionSpec as P

HEADS = 16
score_gain = 2.5
VMEM_LIMIT = 56 << 20


def layer_norm(values):
    centered = values - jnp.mean(values, axis=-1, keepdims=True)
    return centered * lax.rsqrt(jnp.mean(centered * centered, axis=-1, keepdims=True) + 1e-05)


def head_scale(product, head_size):
    width = product.shape[1]
    rows = lax.broadcasted_iota(jnp.int32, (width, width), 0) // head_size
    cols = lax.broadcasted_iota(jnp.int32, (width, width), 1) // head_size
    same = (rows == cols).astype(jnp.float32).astype(jnp.bfloat16)
    squares = product * product
    high = squares.astype(jnp.bfloat16)
    low = (squares - high.astype(jnp.float32)).astype(jnp.bfloat16)
    total = jnp.dot(high, same, preferred_element_type=jnp.float32)
    total = total + jnp.dot(low, same, preferred_element_type=jnp.float32)
    return lax.rsqrt(total * (1.0 / head_size) + 1e-06)


def project_kernel(x_ref, w_ref, *out_refs, plan, head_size):
    width = w_ref.shape[2]
    for j, (place, column, factor) in enumerate(plan):
        product = jnp.dot(x_ref[...], w_ref[j], preferred_element_type=jnp.float32)
        if factor is not None:
            product = product * (head_scale(product, head_size) * factor)
        out_refs[place][:, column * width : (column + 1) * width] = product.astype(jnp.bfloat16)


def project(x, weights, plan, head_size):
    rows, depth = x.shape
    count, _, width = weights.shape
    block = math.gcd(rows, 512)
    places = max(p for p, _, _ in plan) + 1
    widths = [width * sum(p == place for p, _, _ in plan) for place in range(places)]
    return pl.pallas_call(
        functools.partial(project_kernel, plan=plan, head_size=head_size),
        out_shape=[jax.ShapeDtypeStruct((rows, w), jnp.bfloat16) for w in widths],
        grid=(rows // block,),
        in_specs=[
            pl.BlockSpec((block, depth), lambda i: (i, 0)),
            pl.BlockSpec((count, depth, width), lambda i: (0, 0, 0)),
        ],
        out_specs=[pl.BlockSpec((block, w), lambda i: (i, 0)) for w in widths],
        compiler_params=pltpu.CompilerParams(vmem_limit_bytes=VMEM_LIMIT),
        cost_estimate=pl.CostEstimate(
            flops=2 * rows * depth * width * count,
            bytes_accessed=2 * (rows * depth + count * depth * width + rows * width * count),
            transcendentals=rows * width,
        ),
    )(x, weights)


def stack_heads(queries, head_size):
    rows, lanes = queries.shape
    lane = lax.broadcasted_iota(jnp.int32, (rows, lanes), 1) // head_size
    zero = jnp.zeros_like(queries)
    heads = lanes // head_size
    if heads == 1:
        return queries
    return jnp.concatenate([jnp.where(lane == h, queries, zero) for h in range(heads)], axis=0)


def pick_heads(acc_ref, rows, lanes, head_size):
    picked = acc_ref[:rows, :]
    lane = lax.broadcasted_iota(jnp.int32, picked.shape, 1) % lanes // head_size
    for h in range(1, lanes // head_size):
        picked = jnp.where(lane == h, acc_ref[h * rows : (h + 1) * rows, :], picked)
    return picked[:, :lanes], picked[:, lanes:]


def fold_keys(stacked, key_of, value_of, acc_ref, key_count, lanes):
    block = math.gcd(key_count, 512)
    ones = jnp.ones((block, lanes), jnp.bfloat16)
    acc_ref[...] = jnp.zeros_like(acc_ref)

    def step(i, carry):
        rows = pl.ds(pl.multiple_of(i * block, block), block)
        scores = lax.dot_general(
            stacked, key_of(rows), (((1,), (1,)), ((), ())), preferred_element_type=jnp.float32
        )
        weights = jnp.exp2(scores).astype(jnp.bfloat16)
        values = jnp.concatenate([value_of(rows), ones], axis=1)
        acc_ref[...] += jnp.dot(weights, values, preferred_element_type=jnp.float32)
        return carry

    lax.fori_loop(0, key_count // block, step, 0, unroll=True)


def attend_kernel(q_ref, k_ref, v_ref, *refs, head_size, finish):
    acc_ref = refs[-1]
    rows, lanes = q_ref.shape
    fold_keys(
        stack_heads(q_ref[...], head_size),
        lambda r: k_ref[r, :],
        lambda r: v_ref[r, :],
        acc_ref,
        k_ref.shape[0],
        lanes,
    )
    mixed, totals = pick_heads(acc_ref, rows, lanes, head_size)
    if finish:
        refs[0][...] = (mixed / totals).astype(jnp.bfloat16)
    else:
        refs[0][...] = mixed.astype(jnp.bfloat16)
        refs[1][...] = totals


def attend(queries, kv, head_size, finish):
    count, width = queries.shape
    keys = kv.shape[0]
    lanes = min(128, width)
    pairs = width // lanes
    block = math.gcd(count, 512)
    outs = [jax.ShapeDtypeStruct((count, width), jnp.bfloat16)]
    if not finish:
        outs.append(jax.ShapeDtypeStruct((count, width), jnp.float32))
    if width % 128:
        keys_values = (kv[:, :width], kv[:, width:])
        shift = 0
    else:
        keys_values = (kv, kv)
        shift = pairs
    result = pl.pallas_call(
        functools.partial(attend_kernel, head_size=head_size, finish=finish),
        out_shape=outs,
        grid=(pairs, count // block),
        in_specs=[
            pl.BlockSpec((block, lanes), lambda p, i: (i, p)),
            pl.BlockSpec((keys, lanes), lambda p, i: (0, p)),
            pl.BlockSpec((keys, lanes), lambda p, i: (0, p + shift)),
        ],
        out_specs=[pl.BlockSpec((block, lanes), lambda p, i: (i, p))] * len(outs),
        scratch_shapes=[pltpu.VMEM((lanes // head_size * block, 2 * lanes), jnp.float32)],
        compiler_params=pltpu.CompilerParams(vmem_limit_bytes=VMEM_LIMIT),
        cost_estimate=pl.CostEstimate(
            flops=16 * count * keys * width,
            bytes_accessed=2 * (3 * count * width + 2 * keys * width),
            transcendentals=count * keys * width // head_size,
        ),
    )(queries, *keys_values)
    return result


def per_device(
    tri_tokens, image_tokens, cross_q, cross_kv, cross_out, self_qkv, self_out, mlp_in, mlp_out,
    *, tok
):
    width = cross_q.shape[1]
    head_size = tri_tokens.shape[1] // HEADS
    head_count = width // head_size
    query_factor = score_gain / math.sqrt(head_size) * math.log2(math.e)

    def spread(stream):
        return lax.all_gather(layer_norm(stream).astype(jnp.bfloat16), "head", axis=0, tiled=True)

    def collect(operand, weight):
        return lax.psum_scatter(
            jnp.dot(operand, weight, preferred_element_type=jnp.float32).astype(jnp.bfloat16),
            "head",
            scatter_dimension=0,
            tiled=True,
        ).astype(jnp.float32)

    stream_zero = tri_tokens.astype(jnp.float32)
    (queries,) = project(spread(stream_zero), cross_q[None], ((0, 0, query_factor),), head_size)
    (view_kv,) = project(image_tokens, cross_kv, ((0, 0, 1.0), (0, 1, None)), head_size)
    all_queries = lax.all_gather(queries, "tok", axis=0, tiled=True)
    weighted, totals = attend(all_queries, view_kv, head_size, False)
    group = queries.shape[0]
    totals = totals.reshape(tok, group, head_count, head_size)[:, :, :, 0]
    totals = totals.transpose(0, 2, 1).astype(jnp.bfloat16)
    weighted = lax.psum_scatter(weighted, "tok", scatter_dimension=0, tiled=True)
    totals = lax.psum_scatter(totals, "tok", scatter_dimension=0, tiled=True)
    totals = jnp.repeat(totals[0].T.astype(jnp.float32), head_size, axis=1)
    mix = (weighted.astype(jnp.float32) / totals).astype(jnp.bfloat16)
    stream_one = stream_zero + collect(mix, cross_out)
    self_queries, self_kv = project(
        spread(stream_one), self_qkv, ((0, 0, query_factor), (1, 0, 1.0), (1, 1, None)), head_size
    )
    all_kv = lax.all_gather(self_kv, "tok", axis=0, tiled=True)
    (mix,) = attend(self_queries, all_kv, head_size, True)
    stream_two = stream_one + collect(mix, self_out)
    hidden = jax.nn.gelu(
        jnp.dot(spread(stream_two), mlp_in, preferred_element_type=jnp.float32), approximate=True
    ).astype(jnp.bfloat16)
    return (stream_two + collect(hidden, mlp_out)).astype(jnp.bfloat16)


def solution(mesh):
    return jax.shard_map(
        functools.partial(per_device, tok=mesh.shape["tok"]),
        mesh=mesh,
        in_specs=(
            P(("tok", "head"), None),
            P("tok", None),
            P(None, "head"),
            P(None, None, "head"),
            P("head", None),
            P(None, None, "head"),
            P("head", None),
            P(None, "head"),
            P("head", None),
        ),
        out_specs=P(("tok", "head"), None),
        check_vma=False,
    )
```

time: 782 us -> 450 us (0.58)
  matrix products: 285 us -> 10.2 us
  Pallas kernels: 0 us -> 110 us
  local copies, waits for them, and re-layouts: 106 us -> 8.24 us
  waiting for transfers between devices: 350 us -> 254 us
  blocking collectives: 0 us -> 34.8 us
    dot_general x39 -> x0, matrix products: 276 us -> none  [the longest x18 136 us: key_step(): jnp.einsum('qhk,khd->qhd', exp_scores.astype(jnp.bfloat16), key_tile[:, 1...]
    pallas_call x0 -> x5, Pallas kernels: none -> 110 us  [the longest x2 89 us: attend(): pl.pallas_call(functools.partial(attend_kernel, head_size=head_size, fini...]
    unnamed x11 -> x9, waiting for transfers between devices: 59.3 us -> 0.15 us
    reduce_scatter x1, waiting for transfers between devices: 70.3 us -> 19.8 us  [per_device(): lax.psum_scatter(weighted, 'tok', scatter_dimension=0, tiled=True)]
    squeeze x28 -> x0, local copies, waits for them, and re-layouts: 43 us -> none  [the longest x18 32.9 us: one_block(): result, _ = lax.scan(key_step, starting, key_blocks)]
    unnamed x0 -> x1, blocking collectives: none -> 34.8 us
    reshape x2 -> x1, local copies, waits for them, and re-layouts: 21.5 us -> 0.2 us  [per_device(): totals = jnp.repeat(totals[0].T.astype(jnp.float32), head_size, axis=1)]
    unnamed x20 -> x14, local copies, waits for them, and re-layouts: 18.1 us -> 3.67 us
  transfers between devices with their start and end apart: 10 -> 9, of which waited for: 10 -> 9; matrix products, arithmetic and copies ran while one was open for 4% -> 3% of each run, Pallas kernels for 0% -> 3%
where the time goes in v1:
time: 450 us; the launch traced here: 449 us
  waiting for transfers between devices  254 us (56%)
  Pallas kernels  110 us (24%)
  blocking collectives  34.8 us (8%)
  other arithmetic  18.6 us (4%)
  between operations  13.3 us (3%)
  matrix products  10.2 us (2%)
  local copies, waits for them, and re-layouts  8.24 us (2%)
    pallas_call x2, Pallas kernels, attend(): pl.pallas_call(functools.partial(attend_kernel, head_size=head_size, fini...  89 us
    all_gather x1, waiting for transfers between devices, per_device(): all_kv = lax.all_gather(self_kv, 'tok', axis=0, tiled=True)  72.7 us
    reduce_scatter x3, waiting for transfers between devices, collect(): lax.psum_scatter(jnp.dot(operand, weight, preferred_element_type=jnp.floa...  72.3 us
    all_gather x3, waiting for transfers between devices, spread(): lax.all_gather(layer_norm(stream).astype(jnp.bfloat16), 'head', axis=0, t...  53.1 us
    all_gather x1, waiting for transfers between devices, per_device(): all_queries = lax.all_gather(queries, 'tok', axis=0, tiled=True)  35.7 us
    unnamed x1, blocking collectives  34.8 us
    pallas_call x3, Pallas kernels, project(): pl.pallas_call(functools.partial(project_kernel, plan=plan, head_size=hea...  21 us
    reduce_scatter x1, waiting for transfers between devices, per_device(): lax.psum_scatter(weighted, 'tok', scatter_dimension=0, tiled=True)  19.8 us
  transfers between devices with their start and end apart: 9, of which 9 were waited for; matrix products, arithmetic and copies ran while one was open for 3% of the time, Pallas kernels for 3%

profile of v1, /device:TPU:0, one launch (start us, length us, event | category | flops | bytes accessed | tf_op | source)
XLA Modules:
  0.0 449.4 jit_solution(10217410013275304185)
XLA Ops:
  6.5 0.0 copy-start
  6.5 0.0 all-gather.6.cloned.1.call-start
  6.5 1.2 convert_reduce_fusion
  7.8 1.2 fusion.15
  8.9 1.9 fusion.16
  10.8 0.0 all-gather.6.cloned.1.call-update
  10.8 0.0 all-gather.8.cloned.1.call-start
  10.9 19.5 %all-gather.6.cloned.1.call-done.x_ref = bf16[512,1024]{1,0:T(8,128)(2,1)} async-done(((bf16[128,1024]{1,0:T(8,128)(2,1)}), bf16[512,1024]{1,0:T(8,128)(2,1)}) %all-gather.6.cloned.1.call-update) | async-done | bytes 1048592 | tf_op jit(solution)/shard_map/all_gather | solution.py:168
  30.4 2.9 shard_map.91
  33.3 0.0 all-gather.8.cloned.1.call-update
  33.3 0.0 reduce-scatter.5.cloned.1.call-start
  33.4 13.5 %shard_map.92.k_ref.v_ref = bf16[4096,512]{1,0:T(8,128)(2,1)} custom-call(bf16[4096,1024]{1,0:T(8,128)(2,1)} %x_ref.1, bf16[2,1024,256]{2,1,0:T(8,128)(2,1)} %w_ref.2), custom_call_target="tpu_custom_call" | custom-call | flops 4294967296 | bytes 13631488 | tf_op jit(solution)/shard_map/pallas_call | solution.py:49
  46.9 35.7 %all-gather.8.cloned.1.call-done.q_ref = bf16[4096,256]{1,0:T(8,128)(2,1)} async-done(((bf16[512,256]{1,0:T(8,128)(2,1)}), bf16[4096,256]{1,0:T(8,128)(2,1)}) %all-gather.8.cloned.1.call-update) | async-done | bytes 2097168 | tf_op jit(solution)/shard_map/all_gather | solution.py:181
  82.6 77.3 %shard_map.93 = (bf16[4096,256]{1,0:T(8,128)(2,1)}, f32[4096,256]{1,0:T(8,128)}) custom-call(bf16[4096,256]{1,0:T(8,128)(2,1)} %all-gather.8.cloned.1.call-done.q_ref, bf16[4096,512]{1,0:T(8,128)(2,1)} %shard_map.92.k_ref.v_ref, bf16[4096,512]{1,0:T(8,128)(2,1)} %shard_map.92.k_ref.v_ref), custom_call_target="tpu_custom_call" | custom-call | flops 68719476736 | bytes 10485760 | tf_op jit(solution)/shard_map/pallas_call | solution.py:137
  159.9 0.0 copy-start.5
  159.9 0.0 reduce-scatter.5.cloned.1.call-update
  159.9 0.0 reduce-scatter.7.cloned.1.call-start
  159.9 0.6 copy-done.5
  160.5 0.6 dynamic-slice
  161.1 3.7 convert.6
  164.8 4.3 copy.12
  169.1 2.5 copy.15
  171.6 34.8 %all-reduce = bf16[8,4,512]{2,1,0:T(4,128)(2,1)S(1)} all-reduce(bf16[8,4,512]{2,1,0:T(4,128)(2,1)S(1)} %copy.13), channel_id=3, replica_groups=mesh['tok'=8,'head'=4] {'tok'}, use_global_device_ids=true, to_apply=%region_3.0.clone | all-reduce | flops 16384 | bytes 65536
  206.4 0.7 convert_bitcast_fusion
  207.1 0.1 broadcast_in_dim.5
  207.2 0.2 copy.14
  207.4 0.0 copy-start.1
  207.4 19.8 %reduce-scatter.5.cloned.1.call-done = bf16[512,256]{1,0:T(8,128)(2,1)} async-done(((bf16[4096,256]{1,0:T(8,128)(2,1)}), bf16[512,256]{1,0:T(8,128)(2,1)}) %reduce-scatter.5.cloned.1.call-update) | async-done | bytes 262160 | tf_op jit(solution)/shard_map/reduce_scatter | solution.py:186
  227.2 2.5 convolution_convert_fusion.2
  229.7 0.0 reduce-scatter.7.cloned.1.call-update
  229.7 0.0 all-gather.10.cloned.1.call-start
  229.8 23.9 %reduce-scatter.7.cloned.1.call-done = bf16[128,1024]{1,0:T(8,128)(2,1)} async-done(((bf16[512,1024]{1,0:T(8,128)(2,1)}), bf16[128,1024]{1,0:T(8,128)(2,1)}) %reduce-scatter.7.cloned.1.call-update) | async-done | bytes 262160 | tf_op jit(solution)/shard_map/reduce_scatter | solution.py:171
  253.7 0.0 copy-done.1
  253.7 1.1 fusion.17
  254.8 1.2 multiply_reduce_fusion.1
  256.0 1.8 multiply_convert_fusion.1
  257.8 0.0 all-gather.10.cloned.1.call-update
  257.8 0.0 all-gather.12.cloned.1.call-start
  257.9 16.8 %all-gather.10.cloned.1.call-done.x_ref = bf16[512,1024]{1,0:T(8,128)(2,1)} async-done(((bf16[128,1024]{1,0:T(8,128)(2,1)}), bf16[512,1024]{1,0:T(8,128)(2,1)}) %all-gather.10.cloned.1.call-update) | async-done | bytes 1048592 | tf_op jit(solution)/shard_map/all_gather | solution.py:168
  274.7 4.6 %shard_map.94 = (bf16[512,256]{1,0:T(8,128)(2,1)}, bf16[512,512]{1,0:T(8,128)(2,1)}) custom-call(bf16[512,1024]{1,0:T(8,128)(2,1)} %all-gather.10.cloned.1.call-done.x_ref, bf16[3,1024,256]{2,1,0:T(8,128)(2,1)} %w_ref.3), custom_call_target="tpu_custom_call" | custom-call | flops 805306368 | bytes 3407872 | tf_op jit(solution)/shard_map/pallas_call | solution.py:49
  279.2 0.0 all-gather.12.cloned.1.call-update
  279.3 0.2 reduce-scatter.9.cloned.1.call-start
  279.5 72.7 %all-gather.12.cloned.1.call-done.k_ref.v_ref = bf16[4096,512]{1,0:T(8,128)(2,1)} async-done(((bf16[512,512]{1,0:T(8,128)(2,1)}), bf16[4096,512]{1,0:T(8,128)(2,1)}) %all-gather.12.cloned.1.call-update) | async-done | bytes 4194320 | tf_op jit(solution)/shard_map/all_gather | solution.py:194
  352.2 0.0 copy-start.4
  352.2 11.7 %shard_map.95 = bf16[512,256]{1,0:T(8,128)(2,1)} custom-call(bf16[512,256]{1,0:T(8,128)(2,1)} %get-tuple-element.11.q_ref, bf16[4096,512]{1,0:T(8,128)(2,1)} %all-gather.12.cloned.1.call-done.k_ref.v_ref, bf16[4096,512]{1,0:T(8,128)(2,1)} %all-gather.12.cloned.1.call-done.k_ref.v_ref), custom_call_target="tpu_custom_call" | custom-call | flops 8589934592 | bytes 4980736 | tf_op jit(solution)/shard_map/pallas_call | solution.py:137
  363.9 0.0 copy-done.4
  363.9 2.4 convolution_convert_fusion.1
  366.3 0.0 reduce-scatter.9.cloned.1.call-update
  366.3 0.0 all-gather.14.cloned.1.call-start
  366.4 23.4 %reduce-scatter.9.cloned.1.call-done = bf16[128,1024]{1,0:T(8,128)(2,1)} async-done(((bf16[512,1024]{1,0:T(8,128)(2,1)}), bf16[128,1024]{1,0:T(8,128)(2,1)}) %reduce-scatter.9.cloned.1.call-update) | async-done | bytes 262160 | tf_op jit(solution)/shard_map/reduce_scatter | solution.py:171
  389.8 0.0 copy-done.2
  389.8 1.1 fusion.22
  390.9 1.2 multiply_reduce_fusion
  392.1 1.8 multiply_convert_fusion
  393.9 0.0 all-gather.14.cloned.1.call-update
  393.9 0.0 copy-start.3
  393.9 0.0 reduce-scatter.11.cloned.1.call-start
  394.0 16.8 %all-gather.14.cloned.1.call-done = bf16[512,1024]{1,0:T(8,128)(2,1)} async-done(((bf16[128,1024]{1,0:T(8,128)(2,1)}), bf16[512,1024]{1,0:T(8,128)(2,1)}) %all-gather.14.cloned.1.call-update) | async-done | bytes 1048592 | tf_op jit(solution)/shard_map/all_gather | solution.py:168
  410.8 0.0 copy-done
  410.8 5.3 %convolution_convert_fusion = bf16[512,1024]{1,0:T(8,128)(2,1)} fusion(bf16[1024,1024]{1,0:T(8,128)(2,1)S(1)} %copy-done, bf16[512,1024]{1,0:T(8,128)(2,1)} %all-gather.14.cloned.1.call-done, bf16[1024,1024]{1,0:T(8,128)(2,1)} %param.16), kind=kOutput, calls=%fused_computation.9 | convolution fusion | flops 2152726528 | bytes 6291456 | tf_op jit(solution)/shard_map/dot_general | solution.py:172
  416.1 0.0 reduce-scatter.11.cloned.1.call-update
  416.1 24.9 %reduce-scatter.11.cloned.1.call-done = bf16[128,1024]{1,0:T(8,128)(2,1)} async-done(((bf16[512,1024]{1,0:T(8,128)(2,1)}), bf16[128,1024]{1,0:T(8,128)(2,1)}) %reduce-scatter.11.cloned.1.call-update) | async-done | bytes 262160 | tf_op jit(solution)/shard_map/reduce_scatter | solution.py:171
  441.0 0.0 copy-done.3
  441.0 1.8 add_convert_fusion
  (9 shorter events, 0.1 us)
Async XLA Ops:
  6.5 404.2 %copy-start = (bf16[1024,1024]{1,0:T(8,128)(2,1)S(1)}, bf16[1024,1024]{1,0:T(8,128)(2,1)}, u32[]{:S(2)}) copy-start(bf16[1024,1024]{1,0:T(8,128)(2,1)} %param.17) | copy-start | bytes 6291460
  6.5 23.9 %all-gather.6.cloned.1.call-start = ((), (), s32[]{:S(2)}) async-start(), calls=%async_computation.4 | async-start | bytes 1310720 | tf_op jit(solution)/shard_map/all_gather | solution.py:168
  10.8 71.7 %all-gather.8.cloned.1.call-start = ((), (), s32[]{:S(2)}) async-start(), calls=%async_computation.5 | async-start | bytes 2359296 | tf_op jit(solution)/shard_map/all_gather | solution.py:181
  33.3 193.8 %reduce-scatter.5.cloned.1.call-start = ((), (), s32[]{:S(2)}) async-start(), calls=%async_computation.6 | async-start | bytes 2359296 | tf_op jit(solution)/shard_map/reduce_scatter | solution.py:186
  159.9 0.7 copy-start.5
  159.9 93.8 %reduce-scatter.7.cloned.1.call-start = ((), (), s32[]{:S(2)}) async-start(), calls=%async_computation.7 | async-start | bytes 1310720 | tf_op jit(solution)/shard_map/reduce_scatter | solution.py:171
  207.4 46.4 %copy-start.1 = (bf16[128,1024]{1,0:T(8,128)(2,1)S(1)}, bf16[128,1024]{1,0:T(8,128)(2,1)}, u32[]{:S(2)}) copy-start(bf16[128,1024]{1,0:T(8,128)(2,1)} %param.9) | copy-start | bytes 786436
  229.7 44.9 %all-gather.10.cloned.1.call-start = ((), (), s32[]{:S(2)}) async-start(), calls=%async_computation.8 | async-start | bytes 1310720 | tf_op jit(solution)/shard_map/all_gather | solution.py:168
  257.8 94.4 %all-gather.12.cloned.1.call-start = ((), (), s32[]{:S(2)}) async-start(), calls=%async_computation.9 | async-start | bytes 4718592 | tf_op jit(solution)/shard_map/all_gather | solution.py:194
  279.3 110.5 %reduce-scatter.9.cloned.1.call-start = ((), (), s32[]{:S(2)}) async-start(), calls=%async_computation.10 | async-start | bytes 1310720 | tf_op jit(solution)/shard_map/reduce_scatter | solution.py:171
  352.2 11.7 %copy-start.4 = (bf16[256,1024]{1,0:T(8,128)(2,1)S(1)}, bf16[256,1024]{1,0:T(8,128)(2,1)}, u32[]{:S(2)}) copy-start(bf16[256,1024]{1,0:T(8,128)(2,1)} %param.15) | copy-start | bytes 1572868
  363.9 25.9 %copy-start.2 = (bf16[128,1024]{1,0:T(8,128)(2,1)S(1)}, bf16[128,1024]{1,0:T(8,128)(2,1)}, u32[]{:S(2)}) copy-start(bf16[128,1024]{1,0:T(8,128)(2,1)} %reduce-scatter.7.cloned.1.call-done) | copy-start | bytes 786436
  366.3 44.5 %all-gather.14.cloned.1.call-start = ((), (), s32[]{:S(2)}) async-start(), calls=%async_computation.11 | async-start | bytes 1310720 | tf_op jit(solution)/shard_map/all_gather | solution.py:168
  393.9 47.1 %copy-start.3 = (bf16[128,1024]{1,0:T(8,128)(2,1)S(1)}, bf16[128,1024]{1,0:T(8,128)(2,1)}, u32[]{:S(2)}) copy-start(bf16[128,1024]{1,0:T(8,128)(2,1)} %reduce-scatter.9.cloned.1.call-done) | copy-start | bytes 786436
  393.9 47.1 %reduce-scatter.11.cloned.1.call-start = ((), (), s32[]{:S(2)}) async-start(), calls=%async_computation.12 | async-start | bytes 1310720 | tf_op jit(solution)/shard_map/reduce_scatter | solution.py:171
Sparse Core Ops, SparseCore 0:
  11.0 19.4 all-gather.5
  33.4 49.0 all-gather.7
  160.0 67.1 reduce-scatter.4
  229.9 23.8 reduce-scatter.6
  257.9 16.6 all-gather.9
  279.4 72.7 all-gather.11
  366.4 23.2 reduce-scatter.8
  394.0 16.6 all-gather.13
  416.2 24.7 reduce-scatter.10
